TPU v7x, 128 devices: a whole 4x4x4 slice. The times are simulated.
128 devices in a mesh: seq: 16 (over z, y_hi, core), tensor: 8 (over x, y_lo).
Axes of the slice: x: 4, y: 4 (y_hi: 2, y_lo: 2; y = y_hi * 2 + y_lo), z: 4, core: 2. Of those that a mesh axis runs over, the one named last changes fastest.
Arguments:
- queries: bfloat16 [3, 48, 40, 5120], P(None, 'seq', None, 'tensor'), may hold values from -16 to 16
- keys_values: bfloat16 [2, 3, 48, 40, 5120], P(None, None, 'seq', None, 'tensor'), may hold values from -16 to 16
- out_weight: bfloat16 [5120, 5120], P('tensor'), may hold values from -0.078125 to 0.078125
- grad_out: bfloat16 [3, 48, 40, 5120], P(None, 'seq', 'tensor'), may hold values from -6 to 6
- window: int32 [40, 3], P('tensor'), may hold values from 0 to 3, as said below
- block_mask: int32 [1, 16, 5, 63], replicated, may hold values from 0 to 1, as said below
Outputs:
- layer_out: bfloat16 [3, 48, 40, 5120], P(None, 'seq', 'tensor')
- grad_queries: bfloat16 [3, 48, 40, 5120], P(None, 'seq', None, 'tensor')
- grad_keys_values: bfloat16 [2, 3, 48, 40, 5120], P(None, None, 'seq', None, 'tensor')
- grad_weight: bfloat16 [5120, 5120], P('tensor', 'seq')
Inputs may be any that keep to these rules, and one draw needn't show every extreme that they name: `window`: in every group of 5 consecutive heads one head has the reach (1, 1, 3). `block_mask`: the middle entry of every tile's row (the tile itself) is 1.
All inputs are finite; a program needn't handle non-finite values.
Results may differ from a plain program's by a relative error of at most 0.014.
Values may be sent and summed in bfloat16 or wider, within the bound.
No kernel may reach another device: no remote copies, remote signals or barrier semaphores. Data moves between devices by JAX's collectives and lax.ppermute only.
A program may use at most 128 MiB of HBM per device.

v0:
```python
import jax
import jax.numpy as jnp
from jax import lax
from jax.sharding import PartitionSpec as P

HEAD_DIM = 128
TILE_F = 3
TILE_H = 3
TILE_W = 8
REACH_F = 1
REACH_H = 1
REACH_W = 3
OFFSETS = 63


def padded(cells, sides, width):
    for axis, dim in sides:
        count = lax.axis_size(axis)
        ends = count - 1
        head = lax.slice_in_dim(cells, 0, width, axis=dim)
        tail = lax.slice_in_dim(cells, cells.shape[dim] - width, cells.shape[dim], axis=dim)
        cells = jnp.concatenate(
            [
                lax.ppermute(tail, axis, [(i, (i + 1) % count) for i in range(ends)]),
                cells,
                lax.ppermute(head, axis, [((i + 1) % count, i) for i in range(ends)]),
            ],
            axis=dim,
        )
    return cells


def from_behind(value, axis, steps):
    count = lax.axis_size(axis)
    initial, last = (max(0, -steps), min(count, count - steps))
    return lax.ppermute(value, axis, [(source, source + steps) for source in range(initial, last)])


def tile_order(grid):
    frames, height, columns, channels = grid.shape
    shaped = grid.reshape(
        frames // TILE_F, TILE_F, height // TILE_H, TILE_H, columns // TILE_W, TILE_W, channels
    )
    return shaped.transpose(0, 2, 4, 1, 3, 5, 6).reshape(-1, channels)


def grid_order(flat_rows, frames, height, columns):
    channels = flat_rows.shape[-1]
    shaped = flat_rows.reshape(
        frames // TILE_F, height // TILE_H, columns // TILE_W, TILE_F, TILE_H, TILE_W, channels
    )
    return shaped.transpose(0, 3, 1, 4, 2, 5, 6).reshape(frames, height, columns, channels)


def tile_coords(frames, height, columns, first_row):
    frame_count = frames // TILE_F
    row_count = height // TILE_H
    column_count = columns // TILE_W
    linear = jnp.arange(frame_count * row_count * column_count, dtype=jnp.int32)
    return (
        linear // (row_count * column_count),
        linear // column_count % row_count + first_row,
        linear % column_count,
    )


def allowed_mask(reach_row, mask_rows, query_tiles, key_tiles, row_tiles):
    delta_f = key_tiles[0][None, :] - query_tiles[0][:, None]
    delta_h = key_tiles[1][None, :] - query_tiles[1][:, None]
    delta_w = key_tiles[2][None, :] - query_tiles[2][:, None]
    inside = (
        (jnp.abs(delta_f) <= reach_row[0])
        & (jnp.abs(delta_h) <= reach_row[1])
        & (jnp.abs(delta_w) <= reach_row[2])
    )
    inside = inside & ((key_tiles[1] >= 0) & (key_tiles[1] < row_tiles))[None, :]
    offset = (
        ((delta_f + REACH_F) * (2 * REACH_H + 1) + delta_h + REACH_H) * (2 * REACH_W + 1)
        + delta_w
        + REACH_W
    )
    mask_bits = jnp.sum(
        jnp.where(
            offset[:, :, None] == jnp.arange(OFFSETS, dtype=jnp.int32), mask_rows[:, None, :], 0
        ),
        axis=-1,
    )
    tiles_ok = inside & (mask_bits > 0)
    tile_size = TILE_F * TILE_H * TILE_W
    query_count, key_count = tiles_ok.shape
    spread = jnp.broadcast_to(
        tiles_ok[:, None, :, None], (query_count, tile_size, key_count, tile_size)
    )
    return spread.reshape(query_count * tile_size, key_count * tile_size)


def split_heads(flat_rows):
    return flat_rows.reshape(flat_rows.shape[0], -1, HEAD_DIM).transpose(1, 0, 2)


def join_heads(stacked):
    return stacked.transpose(1, 0, 2).reshape(stacked.shape[1], -1)


def head_forward(q_rows, k_rows, v_rows, allowed):
    scores = jnp.dot(q_rows, k_rows.T, preferred_element_type=jnp.float32) * HEAD_DIM ** (-0.5)
    scores = jnp.where(allowed, scores, -jnp.inf)
    row_max = jnp.max(scores, axis=1)
    weights = jnp.exp(scores - row_max[:, None])
    row_sum = jnp.sum(weights, axis=1)
    probs = weights / row_sum[:, None]
    attended = jnp.dot(
        probs.astype(jnp.bfloat16), v_rows, preferred_element_type=jnp.float32
    ).astype(jnp.bfloat16)
    return (attended, row_max, row_sum)


def head_backward(q_rows, k_rows, v_rows, grad_rows, allowed, row_max, row_sum, row_delta):
    scores = jnp.dot(q_rows, k_rows.T, preferred_element_type=jnp.float32) * HEAD_DIM ** (-0.5)
    scores = jnp.where(allowed, scores, -jnp.inf)
    probs = jnp.exp(scores - row_max[:, None]) / jnp.maximum(row_sum, 1.0)[:, None]
    rounded = probs.astype(jnp.bfloat16)
    grad_values = jnp.dot(rounded.T, grad_rows, preferred_element_type=jnp.float32)
    grad_probs = jnp.dot(grad_rows, v_rows.T, preferred_element_type=jnp.float32)
    row_delta = jnp.sum(probs * grad_probs, axis=1)
    grad_scores = (probs * (grad_probs - row_delta[:, None]) * HEAD_DIM ** (-0.5)).astype(
        jnp.bfloat16
    )
    grad_queries = jnp.dot(grad_scores, k_rows, preferred_element_type=jnp.float32)
    grad_keys = jnp.dot(grad_scores.T, q_rows, preferred_element_type=jnp.float32)
    return (grad_queries, grad_keys, grad_values, row_delta)


def shards(queries, keys_values, out_weight, grad_out, window, block_mask):
    frames, tile_rows, columns, channels = queries.shape
    model_width = grad_out.shape[3]
    local_columns = grad_out.shape[2]
    row_tiles = lax.axis_size("seq")
    seq_place = lax.axis_index("seq")
    padded_kv = padded(keys_values, (("seq", 2),), TILE_H)
    own_tiles = tile_coords(frames, tile_rows, columns, seq_place)
    wide_tiles = tile_coords(frames, 3 * tile_rows, columns, seq_place - 1)
    own_mask = lax.dynamic_slice_in_dim(block_mask, seq_place, 1, 1).reshape(-1, OFFSETS)
    q_heads = split_heads(tile_order(queries))
    k_heads = split_heads(tile_order(padded_kv[0]))
    v_heads = split_heads(tile_order(padded_kv[1]))

    def forward_one(inputs):
        q_rows, k_rows, v_rows, reach_row = inputs
        allowed = allowed_mask(reach_row, own_mask, own_tiles, wide_tiles, row_tiles)
        return head_forward(q_rows, k_rows, v_rows, allowed)

    attended, row_max, row_sum = lax.map(forward_one, (q_heads, k_heads, v_heads, window))
    attn_grid = grid_order(join_heads(attended), frames, tile_rows, columns)
    flat_rows = attn_grid.transpose(2, 0, 1, 3).reshape(-1, channels)
    mixed_sum = lax.psum_scatter(
        jnp.dot(flat_rows, out_weight, preferred_element_type=jnp.float32)
        .reshape(local_columns * lax.axis_size("tensor"), frames, tile_rows, model_width)
        .astype(jnp.bfloat16),
        "tensor",
        scatter_dimension=0,
        tiled=True,
    ).astype(jnp.float32)
    layer_out = mixed_sum.transpose(1, 2, 0, 3).astype(jnp.bfloat16)
    pieces = lax.all_gather(grad_out, "tensor", axis=2, tiled=True)
    amount = pieces.shape[2]
    flat_piece = pieces.reshape(-1, model_width)
    partial_value = jnp.dot(flat_piece, out_weight.T, preferred_element_type=jnp.float32).astype(
        jnp.bfloat16
    )
    grad_attn = partial_value.reshape(frames, tile_rows, amount, channels)
    used_rows = attn_grid.reshape(-1, channels)
    weight_term = jnp.dot(used_rows.T, flat_piece, preferred_element_type=jnp.float32)
    grad_attn, weight_term = (grad_attn, weight_term)
    grad_weight = lax.psum_scatter(
        weight_term.astype(jnp.bfloat16), "seq", scatter_dimension=1, tiled=True
    )
    g_heads = split_heads(tile_order(grad_attn))

    def backward_one(inputs):
        q_rows, k_rows, v_rows, grad_rows, reach_row, head_max, head_sum = inputs
        allowed = allowed_mask(reach_row, own_mask, own_tiles, wide_tiles, row_tiles)
        result = head_backward(q_rows, k_rows, v_rows, grad_rows, allowed, head_max, head_sum, None)
        return (result[0], result[1], result[2])

    grad_q, grad_k, grad_v = lax.map(
        backward_one, (q_heads, k_heads, v_heads, g_heads, window, row_max, row_sum)
    )
    wide_grads = jnp.stack(
        [
            grid_order(join_heads(grad_k), frames, 3 * tile_rows, columns),
            grid_order(join_heads(grad_v), frames, 3 * tile_rows, columns),
        ]
    )
    from_below = from_behind(wide_grads[:, :, :tile_rows].astype(jnp.bfloat16), "seq", -1).astype(
        jnp.float32
    )
    from_above = from_behind(
        wide_grads[:, :, 2 * tile_rows :].astype(jnp.bfloat16), "seq", 1
    ).astype(jnp.float32)
    grad_kv = (wide_grads[:, :, tile_rows : 2 * tile_rows] + from_below + from_above).astype(
        jnp.bfloat16
    )
    grad_queries = grid_order(join_heads(grad_q), frames, tile_rows, columns).astype(jnp.bfloat16)
    return (layer_out, grad_queries, grad_kv, grad_weight)


def solution(mesh):
    return jax.shard_map(
        shards,
        mesh=mesh,
        in_specs=(
            P(None, "seq", None, "tensor"),
            P(None, None, "seq", None, "tensor"),
            P("tensor", None),
            P(None, "seq", "tensor", None),
            P("tensor", None),
            P(),
        ),
        out_specs=(
            P(None, "seq", "tensor", None),
            P(None, "seq", None, "tensor"),
            P(None, None, "seq", None, "tensor"),
            P("tensor", "seq"),
        ),
        check_vma=False,
    )
```

profile of v0, /device:TPU:0, one launch (start us, length us, event | category | flops | bytes accessed | tf_op | source)
XLA Modules:
  0.0 469.2 jit_solution(18415698256053256040)
XLA Ops:
  7.2 2.4 collective-permute-start
  20.9 3.2 reshape_reshape.29
  25.4 3.2 reshape_reshape.30
  29.9 47.5 %while.32 = (s32[]{:T(128)}, bf16[5,360,128]{2,1,0:T(8,128)(2,1)}, f32[5,360]{1,0:T(8,128)S(1)}, f32[5,360]{1,0:T(8,128)S(1)}, s32[5,3]{0,1:T(4,128)S(1)}, /*ind...) while((s32[]{:T(128)}, bf16[5,360,128]{2,1,0:T(8,128)(2,1)}, ...), condition=%wide.region_4.5_spmd.clone.clone, body=%wide.region_0.4_spmd.clone.clone.sunk | while | flops 202237504 | bytes 7008191 | solution.py:153
  37.0 2.2 fusion.148
  46.5 2.2 fusion.148
  56.0 2.2 fusion.148
  75.0 2.2 fusion.148
  79.1 5.9 %convolution_convert_fusion.2 = bf16[40,3,3,5120]{3,0,2,1:T(8,128)(2,1)S(1)} fusion(bf16[640,5120]{1,0:T(8,128)(2,1)} %param.12, bf16[1,1,5,3,3,8,640]{6,5,4,3,2,1,0:T(8,128)(2,1)S(1)} %reshape_reshape.31), kind=kOutput, calls=%fused_computation.138 | convolution fusion | flops 2361139200 | bytes 10700800 | tf_op jit(solution)/shard_map/dot_general | solution.py:157
  85.0 5.3 %copy.87 = bf16[40,3,3,5120]{3,2,1,0:T(4,128)(2,1)} copy(bf16[40,3,3,5120]{3,0,2,1:T(8,128)(2,1)S(1)} %convolution_convert_fusion.2) | data formatting | bytes 7372800 | tf_op jit(solution)/shard_map/convert_element_type | solution.py:159
  90.7 31.7 %all-gather.2.cloned.1.call-done = bf16[3,3,40,5120]{3,1,0,2:T(4,128)(2,1)} async-done(((bf16[3,3,5,5120]{3,1,0,2:T(4,128)(2,1)}), bf16[3,3,40,5120]{3,1,0,2:T(4,128)(2,1)}) %all-gather.2.cloned.1.call-update) | async-done | bytes 3686416 | tf_op jit(solution)/shard_map/all_gather | solution.py:165
  122.4 3.8 copy.89
  126.2 6.6 %convolution_convert_fusion.3 = bf16[360,640]{1,0:T(8,128)(2,1)S(1)} fusion(bf16[360,5120]{1,0:T(8,128)(2,1)S(1)} %bitcast.188, bf16[640,5120]{1,0:T(8,128)(2,1)} %param.12), kind=kOutput, calls=%fused_computation.150 | convolution fusion | flops 2359526400 | bytes 10700800 | tf_op jit(solution)/shard_map/dot_general | solution.py:168
  133.5 8.7 %convolution_convert_fusion.1 = bf16[640,5120]{0,1:T(8,128)(2,1)} fusion(bf16[360,640]{1,0:T(8,128)(2,1)S(1)} %bitcast.198, bf16[360,5120]{1,0:T(8,128)(2,1)} %bitcast.189), kind=kOutput, calls=%fused_computation.137 | convolution fusion | flops 2362572800 | bytes 10700800 | tf_op jit(solution)/shard_map/dot_general | solution.py:173
  143.2 64.0 %while.33 = (s32[]{:T(128)}, bf16[5,360,128]{2,1,0:T(8,128)(2,1)S(1)}, f32[5,1080,128]{2,1,0:T(8,128)}, f32[5,1080,128]{2,1,0:T(8,128)}, s32[5,3]{0,1:T(4,128)S(...) while((s32[]{:T(128)}, ...), condition=%wide.region_9.10_spmd.clone.clone, body=%wide.region_6.9_spmd.clone.clone.sunk | while | flops 501956928 | bytes 16065771 | solution.py:186
  207.2 6.3 %copy.99 = f32[1080,5,128]{2,1,0:T(8,128)} copy(f32[1080,5,128]{2,0,1:T(8,128)} %bitcast.192) | data formatting | bytes 5529600 | tf_op jit(solution)/shard_map/transpose | solution.py:102
  213.5 4.8 %reshape_reshape.35 = f32[1,3,5,3,3,8,640]{6,5,4,3,2,1,0:T(8,128)} reshape(f32[1080,5,128]{2,1,0:T(8,128)} %copy.99) | data formatting | bytes 5529600 | tf_op jit(solution)/shard_map/reshape;reshape | solution.py:49
  221.0 5.3 %copy.97 = f32[1080,5,128]{2,1,0:T(8,128)} copy(f32[1080,5,128]{2,0,1:T(8,128)S(1)} %bitcast.193) | data formatting | bytes 5529600 | tf_op jit(solution)/shard_map/transpose | solution.py:102
  226.3 4.8 %reshape_reshape.34 = f32[1,3,5,3,3,8,640]{6,5,4,3,2,1,0:T(8,128)} reshape(f32[1080,5,128]{2,1,0:T(8,128)} %copy.97) | data formatting | bytes 5529600 | tf_op jit(solution)/shard_map/reshape;reshape | solution.py:49
  237.2 8.0 %collective-permute-start.3 = (bf16[2,3,3,40,640]{4,3,2,1,0:T(8,128)(2,1)}, bf16[2,3,3,40,640]{4,3,2,1,0:T(8,128)(2,1)}, u32[]{:S(2)}, u32[]{:S(2)}) collective-permute-start(bf16[2,3,3,40,640]{4,3,2,1,0:T(8,128)(2,1)} %get-tuple-element.560), channel_id=1, source_target_pairs={{0,8},{8,16},{16,24},{24,32},{32,40},{40,48},{48,56},{56,64},{64,7... | collective-permute-start | bytes 2764808 | tf_op jit(solution)/shard_map/ppermute | solution.py:36
  246.5 108.6 %all-reduce.3.cloned.1.call-done = bf16[40,3,3,5120]{3,2,1,0:T(4,128)(2,1)} async-done(((bf16[40,3,3,5120]{3,2,1,0:T(4,128)(2,1)}), bf16[40,3,3,5120]{3,2,1,0:T(4,128)(2,1)}) %all-reduce.3.cloned.1.call-update) | async-done | bytes 3686416
  358.5 2.3 convert_element_type.57
  362.7 3.0 fusion.102
  365.7 97.0 %reduce-scatter.2.cloned.1.call-done = bf16[640,320]{0,1:T(8,128)(2,1)} async-done(((bf16[640,5120]{0,1:T(8,128)(2,1)}), bf16[640,320]{0,1:T(8,128)(2,1)}) %reduce-scatter.2.cloned.1.call-update) | async-done | bytes 409616 | tf_op jit(solution)/shard_map/reduce_scatter | solution.py:175
  (235 shorter events, 134.1 us)
Async XLA Ops:
  7.2 6.7 %copy-start = (bf16[3,3,40,640]{3,2,1,0:T(8,128)(2,1)S(1)}, bf16[3,3,40,640]{3,2,1,0:T(8,128)(2,1)}, u32[]{:S(2)}) copy-start(bf16[3,3,40,640]{3,2,1,0:T(8,128)(2,1)} %param.10) | copy-start | bytes 1382404
  7.2 115.2 %all-gather.2.cloned.1.call-start = ((), (), s32[]{:S(2)}) async-start(), calls=%async_computation.1 | async-start | bytes 5529600 | tf_op jit(solution)/shard_map/all_gather | solution.py:165
  7.2 7.3 %collective-permute-start = (bf16[2,3,3,40,640]{4,3,2,1,0:T(8,128)(2,1)}, bf16[2,3,3,40,640]{4,3,2,1,0:T(8,128)(2,1)}, u32[]{:S(2)}, u32[]{:S(2)}) collective-permute-start(bf16[2,3,3,40,640]{4,3,2,1,0:T(8,128)(2,1)} %param.11), channel_id=1, source_target_pairs={{0,8},{8,16},{16,24},{24,32},{32,40},{40,48},{48,56},{56,64},{64,7... | collective-permute-start | bytes 2764808 | tf_op jit(solution)/shard_map/ppermute | solution.py:24
  9.6 7.3 %collective-permute-start.1 = (bf16[2,3,3,40,640]{4,3,2,1,0:T(8,128)(2,1)}, bf16[2,3,3,40,640]{4,3,2,1,0:T(8,128)(2,1)}, u32[]{:S(2)}, u32[]{:S(2)}) collective-permute-start(bf16[2,3,3,40,640]{4,3,2,1,0:T(8,128)(2,1)} %param.11), channel_id=1, source_target_pairs={{8,0},{16,8},{24,16},{32,24},{40,32},{48,40},{56,48},{64,56},{72,6... | collective-permute-start | bytes 2764808 | tf_op jit(solution)/shard_map/ppermute | solution.py:26
  13.0 342.1 %all-reduce.3.cloned.1.call-start = ((), (), s32[]{:S(2)}) async-start(), calls=%async_computation.3 | async-start | bytes 9830400
  13.9 1.9 copy-start.5
  28.6 1.3 copy-start.9
  90.4 372.3 %reduce-scatter.2.cloned.1.call-start = ((), (), s32[]{:S(2)}) async-start(), calls=%async_computation.2 | async-start | bytes 6963200 | tf_op jit(solution)/shard_map/reduce_scatter | solution.py:175
  126.2 6.7 %copy-start.3 = (bf16[3,3,40,5120]{3,2,1,0:T(8,128)(2,1)}, bf16[3,3,40,5120]{3,2,1,0:T(8,128)(2,1)S(1)}, u32[]{:S(2)}) copy-start(bf16[3,3,40,5120]{3,2,1,0:T(8,128)(2,1)S(1)} %copy.89) | copy-start | bytes 11059204
  142.2 1.0 copy-start.6
  207.2 6.3 %copy-start.7 = (bf16[5,360,128]{2,1,0:T(8,128)(2,1)}, bf16[5,360,128]{2,1,0:T(8,128)(2,1)S(1)}, u32[]{:S(2)}) copy-start(bf16[5,360,128]{2,1,0:T(8,128)(2,1)S(1)} %get-tuple-element.204) | copy-start | bytes 1382404
  218.4 2.6 copy-start.4
  233.0 1.5 copy-start.2
  234.6 10.7 %copy-start.10 = (u32[128]{0:T(128)S(1)}, u32[128]{0:T(128)}, u32[]{:S(2)}) copy-start(u32[128]{0:T(128)} %constant.149) | copy-start | bytes 1540
  234.6 122.9 %copy-start.8 = (bf16[5,360,128]{2,1,0:T(8,128)(2,1)S(1)}, bf16[5,360,128]{2,1,0:T(8,128)(2,1)}, u32[]{:S(2)}) copy-start(bf16[5,360,128]{2,1,0:T(8,128)(2,1)} %copy-done.7) | copy-start | bytes 1382404
  236.0 126.7 %collective-permute-start.2 = (bf16[2,3,3,40,640]{4,3,2,1,0:T(8,128)(2,1)}, bf16[2,3,3,40,640]{4,3,2,1,0:T(8,128)(2,1)}, u32[]{:S(2)}, u32[]{:S(2)}) collective-permute-start(bf16[2,3,3,40,640]{4,3,2,1,0:T(8,128)(2,1)} %get-tuple-element.559), channel_id=1, source_target_pairs={{8,0},{16,8},{24,16},{32,24},{40,32},{48,40},{56,48},{64,56},{72,6... | collective-permute-start | bytes 2764808 | tf_op jit(solution)/shard_map/ppermute | solution.py:36
  237.2 125.4 %collective-permute-start.3 = (bf16[2,3,3,40,640]{4,3,2,1,0:T(8,128)(2,1)}, bf16[2,3,3,40,640]{4,3,2,1,0:T(8,128)(2,1)}, u32[]{:S(2)}, u32[]{:S(2)}) collective-permute-start(bf16[2,3,3,40,640]{4,3,2,1,0:T(8,128)(2,1)} %get-tuple-element.560), channel_id=1, source_target_pairs={{0,8},{8,16},{16,24},{24,32},{32,40},{40,48},{48,56},{56,64},{64,7... | collective-permute-start | bytes 2764808 | tf_op jit(solution)/shard_map/ppermute | solution.py:36
  360.8 101.9 %copy-start.1 = (bf16[3,3,40,640]{3,2,1,0:T(8,128)(2,1)S(1)}, bf16[3,3,40,640]{3,2,1,0:T(8,128)(2,1)}, u32[]{:S(2)}) copy-start(bf16[3,3,40,640]{3,2,1,0:T(8,128)(2,1)} %param.10) | copy-start | bytes 1382404
Sparse Core Ops, SparseCore 0:
  13.2 109.1 all-gather.1
  124.9 230.1 all-reduce.2
  359.9 102.7 reduce-scatter.1
where the time goes:
time: 471 us; the launch traced here: 469 us
  waiting for transfers between devices  238 us (51%)
  local copies, waits for them, and re-layouts  94.9 us (20%)
  matrix products  76.7 us (16%)
  other arithmetic  30.8 us (7%)
  between operations  14.7 us (3%)
  starting transfers between devices  13.3 us (3%)
    unnamed x4, waiting for transfers between devices  109 us
    reduce_scatter x1, waiting for transfers between devices, shards(): lax.psum_scatter(weight_term.astype(jnp.bfloat16), 'seq', scatter_dimensi...  97 us
    all_gather x1, waiting for transfers between devices, shards(): pieces = lax.all_gather(grad_out, 'tensor', axis=2, tiled=True)  31.7 us
    reshape x10, local copies, waits for them, and re-layouts, allowed_mask(): return spread.reshape(query_count * tile_size, key_count * tile_size)  18.6 us
    and x10, other arithmetic, allowed_mask(): tiles_ok = inside & (mask_bits > 0)  13.6 us
    transpose x3, local copies, waits for them, and re-layouts, join_heads(): return stacked.transpose(1, 0, 2).reshape(stacked.shape[1], -1)  12.8 us
    dot_general x5, matrix products, head_forward(): jnp.dot(probs.astype(jnp.bfloat16), v_rows, preferred_element_type=jnp.fl...  11.2 us
    unnamed x32, local copies, waits for them, and re-layouts  10.5 us
  transfers between devices with their start and end apart: 7, of which 4 were waited for; matrix products, arithmetic and copies ran while one was open for 43% of the time, Pallas kernels for 0%

commit v1 on v0

--- a/solution.py
+++ b/solution.py
@@ -2,6 +2,7 @@
 import jax.numpy as jnp
 from jax import lax
 from jax.sharding import PartitionSpec as P
+from jax.lax import all_to_all, axis_size
 
 HEAD_DIM = 128
 TILE_F = 3
@@ -162,7 +163,19 @@
         tiled=True,
     ).astype(jnp.float32)
     layer_out = mixed_sum.transpose(1, 2, 0, 3).astype(jnp.bfloat16)
-    pieces = lax.all_gather(grad_out, "tensor", axis=2, tiled=True)
+
+    def order_the_desk(d0, in_array):
+        return jnp.concatenate(
+            all_to_all(
+                jnp.stack([in_array] * axis_size("tensor"), axis=0),
+                axis_name="tensor",
+                split_axis=0,
+                concat_axis=0,
+            ),
+            axis=d0,
+        )
+
+    pieces = order_the_desk(2, grad_out)
     amount = pieces.shape[2]
     flat_piece = pieces.reshape(-1, model_width)
     partial_value = jnp.dot(flat_piece, out_weight.T, preferred_element_type=jnp.float32).astype(

time: 471 us -> 415 us (0.88); the launches traced: 469 us -> 408 us
  waiting for transfers between devices: 238 us -> 118 us
  starting transfers between devices: 13.3 us -> 55 us
  local copies, waits for them, and re-layouts: 94.9 us -> 110 us
    reduce_scatter x1, waiting for transfers between devices: 97 us -> 0.01 us  [shards(): lax.psum_scatter(weight_term.astype(jnp.bfloat16), 'seq', scatter_dimensi...]
    ppermute x2, starting transfers between devices: 9.29 us -> 45.2 us  [from_behind(): lax.ppermute(value, axis, [(source, source + steps) for source in range(i...]
    all_gather x1 -> x0, waiting for transfers between devices: 31.7 us -> none  [shards(): pieces = lax.all_gather(grad_out, 'tensor', axis=2, tiled=True)]
    another operation x0 -> x2, local copies, waits for them, and re-layouts: none -> 12.5 us  [the longest x1 8.02 us: shards(): flat_piece = pieces.reshape(-1, model_width)]
    unnamed x4 -> x3, waiting for transfers between devices: 109 us -> 118 us
    reshape x0 -> x1, local copies, waits for them, and re-layouts: none -> 6.71 us  [order_the_desk(): jnp.concatenate(all_to_all(jnp.stack([in_array] * axis_size('tensor'), ax...]
    all_to_all x0 -> x1, starting transfers between devices: none -> 5.87 us  [order_the_desk(): all_to_all(jnp.stack([in_array] * axis_size('tensor'), axis=0), axis_name...]
    unnamed x32 -> x31, local copies, waits for them, and re-layouts: 10.5 us -> 9.06 us
  transfers between devices with their start and end apart: 7 -> 7, of which waited for: 4 -> 1; matrix products, arithmetic and copies ran while one was open for 43% -> 53% of each run, Pallas kernels for 0% -> 0%
where the time goes in v1:
time: 415 us; the launch traced here: 408 us
  waiting for transfers between devices  118 us (28%)
  local copies, waits for them, and re-layouts  110 us (27%)
  matrix products  77.3 us (19%)
  starting transfers between devices  55 us (13%)
  other arithmetic  30.5 us (7%)
  between operations  16.7 us (4%)
    unnamed x3, waiting for transfers between devices  118 us
    ppermute x2, starting transfers between devices, from_behind(): lax.ppermute(value, axis, [(source, source + steps) for source in range(i...  45.2 us
    reshape x10, local copies, waits for them, and re-layouts, allowed_mask(): return spread.reshape(query_count * tile_size, key_count * tile_size)  18.6 us
    and x10, other arithmetic, allowed_mask(): tiles_ok = inside & (mask_bits > 0)  13.1 us
    transpose x3, local copies, waits for them, and re-layouts, join_heads(): return stacked.transpose(1, 0, 2).reshape(stacked.shape[1], -1)  12.9 us
    dot_general x5, matrix products, head_forward(): jnp.dot(probs.astype(jnp.bfloat16), v_rows, preferred_element_type=jnp.fl...  11.2 us
    another operation x3, local copies, waits for them, and re-layouts, grid_order(): flat_rows.reshape(frames // TILE_F, height // TILE_H, columns // TILE_W,...  10.3 us
    dot_general x5, matrix products, head_backward(): jnp.dot(q_rows, k_rows.T, preferred_element_type=jnp.float32)  9.48 us
  transfers between devices with their start and end apart: 7, of which 1 were waited for; matrix products, arithmetic and copies ran while one was open for 53% of the time, Pallas kernels for 0%

profile of v1, /device:TPU:0, one launch (start us, length us, event | category | flops | bytes accessed | tf_op | source)
XLA Modules:
  0.0 408.5 jit_solution(12369043092797388487)
XLA Ops:
  8.0 2.4 collective-permute-start
  11.7 4.5 %stack.4 = bf16[8,3,3,5,5120]{4,2,3,1,0:T(4,128)(2,1)} broadcast(bf16[3,3,5,5120]{3,1,2,0:T(4,128)(2,1)} %param.13), dimensions={1,2,3,4} | broadcast | bytes 4147200 | tf_op jit(solution)/shard_map/stack | solution.py:170
  16.2 5.9 %all-to-all-start = ((bf16[8,3,3,5,5120]{4,2,3,1,0:T(4,128)(2,1)}), bf16[8,3,3,5,5120]{4,2,3,1,0:T(4,128)(2,1)}, u32[]{:S(2)}, u32[]{:S(2)}) async-start(bf16[8,3,3,5,5120]{4,2,3,1,0:T(4,128)(2,1)} %stack.4), calls=%async_computation | async-start | bytes 9830400 | tf_op jit(solution)/shard_map/all_to_all | solution.py:169
  29.0 3.6 reshape_reshape.32
  35.7 3.2 reshape_reshape.33
  40.2 46.8 %while.32 = (s32[]{:T(128)}, bf16[5,360,128]{2,1,0:T(8,128)(2,1)}, f32[5,360]{1,0:T(8,128)S(1)}, f32[5,360]{1,0:T(8,128)S(1)}, s32[5,3]{0,1:T(4,128)S(1)}, /*ind...) while((s32[]{:T(128)}, bf16[5,360,128]{2,1,0:T(8,128)(2,1)}, ...), condition=%wide.region_4.5_spmd.clone.clone, body=%wide.region_0.4_spmd.clone.clone.sunk | while | flops 202237504 | bytes 7008183 | solution.py:154
  66.0 2.2 fusion.148
  75.3 2.2 fusion.148
  88.8 5.9 %convolution_convert_fusion.2 = bf16[40,3,3,5120]{3,0,2,1:T(8,128)(2,1)S(1)} fusion(bf16[640,5120]{1,0:T(8,128)(2,1)} %param.12, bf16[1,1,5,3,3,8,640]{6,5,4,3,2,1,0:T(8,128)(2,1)S(1)} %reshape_reshape.34), kind=kOutput, calls=%fused_computation.138 | convolution fusion | flops 2361139200 | bytes 10700800 | tf_op jit(solution)/shard_map/dot_general | solution.py:158
  94.7 5.3 %copy.87 = bf16[40,3,3,5120]{3,2,1,0:T(4,128)(2,1)} copy(bf16[40,3,3,5120]{3,0,2,1:T(8,128)(2,1)S(1)} %convolution_convert_fusion.2) | data formatting | bytes 7372800 | tf_op jit(solution)/shard_map/convert_element_type | solution.py:160
  100.3 6.7 %copy.88 = bf16[3,3,8,5,5120]{4,3,2,1,0:T(8,128)(2,1)} copy(bf16[3,3,8,5,5120]{4,1,3,0,2:T(4,128)(2,1)} %bitcast.16) | data formatting | bytes 7372800 | tf_op jit(solution)/shard_map/reshape | solution.py:168
  107.1 8.0 %reshape_reshape.35 = bf16[360,5120]{1,0:T(8,128)(2,1)} reshape(bf16[3,3,8,5,5120]{4,3,2,1,0:T(8,128)(2,1)} %copy.88) | data formatting | bytes 7372800 | tf_op jit(solution)/shard_map/reshape;reshape | solution.py:180
  115.1 7.0 %convolution_convert_fusion.3 = bf16[360,640]{1,0:T(8,128)(2,1)S(1)} fusion(bf16[360,5120]{1,0:T(8,128)(2,1)} %reshape_reshape.35, bf16[640,5120]{1,0:T(8,128)(2,1)} %param.12), kind=kOutput, calls=%fused_computation.150 | convolution fusion | flops 2359526400 | bytes 10700800 | tf_op jit(solution)/shard_map/dot_general | solution.py:181
  122.8 8.7 %convolution_convert_fusion.1 = bf16[640,5120]{0,1:T(8,128)(2,1)} fusion(bf16[360,640]{1,0:T(8,128)(2,1)S(1)} %bitcast.196, bf16[360,5120]{1,0:T(8,128)(2,1)} %reshape_reshape.35), kind=kOutput, calls=%fused_computation.137 | convolution fusion | flops 2362572800 | bytes 10700800 | tf_op jit(solution)/shard_map/dot_general | solution.py:186
  132.5 65.0 %while.33 = (s32[]{:T(128)}, bf16[5,360,128]{2,1,0:T(8,128)(2,1)S(1)}, f32[5,1080,128]{2,1,0:T(8,128)}, f32[5,1080,128]{2,1,0:T(8,128)}, s32[5,3]{0,1:T(4,128)S(...) while((s32[]{:T(128)}, ...), condition=%wide.region_9.10_spmd.clone.clone, body=%wide.region_6.9_spmd.clone.clone.sunk | while | flops 501956928 | bytes 16065763 | solution.py:199
  197.6 6.4 %copy.96 = f32[1080,5,128]{2,1,0:T(8,128)} copy(f32[1080,5,128]{2,0,1:T(8,128)} %bitcast.190) | data formatting | bytes 5529600 | tf_op jit(solution)/shard_map/transpose | solution.py:103
  204.0 5.0 %reshape_reshape.38 = f32[1,3,5,3,3,8,640]{6,5,4,3,2,1,0:T(8,128)} reshape(f32[1080,5,128]{2,1,0:T(8,128)} %copy.96) | data formatting | bytes 5529600 | tf_op jit(solution)/shard_map/reshape;reshape | solution.py:50
  209.0 2.3 copy.97
  211.9 5.3 %copy.98 = f32[1080,5,128]{2,1,0:T(8,128)} copy(f32[1080,5,128]{2,0,1:T(8,128)S(1)} %bitcast.191) | data formatting | bytes 5529600 | tf_op jit(solution)/shard_map/transpose | solution.py:103
  217.2 4.8 %reshape_reshape.39 = f32[1,3,5,3,3,8,640]{6,5,4,3,2,1,0:T(8,128)} reshape(f32[1080,5,128]{2,1,0:T(8,128)} %copy.98) | data formatting | bytes 5529600 | tf_op jit(solution)/shard_map/reshape;reshape | solution.py:50
  222.0 2.5 copy.99
  228.8 43.9 %collective-permute-start.3 = (bf16[2,3,3,40,640]{4,3,2,1,0:T(8,128)(2,1)}, bf16[2,3,3,40,640]{4,3,2,1,0:T(8,128)(2,1)}, u32[]{:S(2)}, u32[]{:S(2)}) collective-permute-start(bf16[2,3,3,40,640]{4,3,2,1,0:T(8,128)(2,1)} %get-tuple-element.560), channel_id=1, source_target_pairs={{0,8},{8,16},{16,24},{24,32},{32,40},{40,48},{48,56},{56,64},{64,7... | collective-permute-start | bytes 2764808 | tf_op jit(solution)/shard_map/ppermute | solution.py:37
  277.5 3.1 fusion.102
  280.5 117.9 %all-reduce.3.cloned.1.call-done = bf16[40,3,3,5120]{3,2,1,0:T(4,128)(2,1)} async-done(((bf16[40,3,3,5120]{3,2,1,0:T(4,128)(2,1)}), bf16[40,3,3,5120]{3,2,1,0:T(4,128)(2,1)}) %all-reduce.3.cloned.1.call-update) | async-done | bytes 3686416
  (235 shorter events, 134.0 us)
Async XLA Ops:
  8.0 14.9 %copy-start = (bf16[3,3,40,640]{3,2,1,0:T(8,128)(2,1)S(1)}, bf16[3,3,40,640]{3,2,1,0:T(8,128)(2,1)}, u32[]{:S(2)}) copy-start(bf16[3,3,40,640]{3,2,1,0:T(8,128)(2,1)} %param.10) | copy-start | bytes 1382404
  8.0 15.6 %collective-permute-start = (bf16[2,3,3,40,640]{4,3,2,1,0:T(8,128)(2,1)}, bf16[2,3,3,40,640]{4,3,2,1,0:T(8,128)(2,1)}, u32[]{:S(2)}, u32[]{:S(2)}) collective-permute-start(bf16[2,3,3,40,640]{4,3,2,1,0:T(8,128)(2,1)} %param.11), channel_id=1, source_target_pairs={{0,8},{8,16},{16,24},{24,32},{32,40},{40,48},{48,56},{56,64},{64,7... | collective-permute-start | bytes 2764808 | tf_op jit(solution)/shard_map/ppermute | solution.py:25
  10.4 14.6 %collective-permute-start.1 = (bf16[2,3,3,40,640]{4,3,2,1,0:T(8,128)(2,1)}, bf16[2,3,3,40,640]{4,3,2,1,0:T(8,128)(2,1)}, u32[]{:S(2)}, u32[]{:S(2)}) collective-permute-start(bf16[2,3,3,40,640]{4,3,2,1,0:T(8,128)(2,1)} %param.11), channel_id=1, source_target_pairs={{8,0},{16,8},{24,16},{32,24},{40,32},{48,40},{56,48},{64,56},{72,6... | collective-permute-start | bytes 2764808 | tf_op jit(solution)/shard_map/ppermute | solution.py:27
  16.2 84.1 %all-to-all-start = ((bf16[8,3,3,5,5120]{4,2,3,1,0:T(4,128)(2,1)}), bf16[8,3,3,5,5120]{4,2,3,1,0:T(4,128)(2,1)}, u32[]{:S(2)}, u32[]{:S(2)}) async-start(bf16[8,3,3,5,5120]{4,2,3,1,0:T(4,128)(2,1)} %stack.4), calls=%async_computation | async-start | bytes 9830400 | tf_op jit(solution)/shard_map/all_to_all | solution.py:169
  22.1 376.4 %all-reduce.3.cloned.1.call-start = ((), (), s32[]{:S(2)}) async-start(), calls=%async_computation.3 | async-start | bytes 9830400
  23.0 1.9 copy-start.5
  32.6 1.8 copy-start.3
  38.9 1.3 copy-start.9
  100.0 300.8 %reduce-scatter.2.cloned.1.call-start = ((), (), s32[]{:S(2)}) async-start(), calls=%async_computation.2 | async-start | bytes 6963200 | tf_op jit(solution)/shard_map/reduce_scatter | solution.py:188
  131.5 1.0 copy-start.6
  197.6 6.4 %copy-start.7 = (bf16[5,360,128]{2,1,0:T(8,128)(2,1)}, bf16[5,360,128]{2,1,0:T(8,128)(2,1)S(1)}, u32[]{:S(2)}) copy-start(bf16[5,360,128]{2,1,0:T(8,128)(2,1)S(1)} %get-tuple-element.204) | copy-start | bytes 1382404
  209.0 2.9 copy-start.4
  224.5 1.5 copy-start.2
  226.1 46.6 %copy-start.10 = (u32[128]{0:T(128)S(1)}, u32[128]{0:T(128)}, u32[]{:S(2)}) copy-start(u32[128]{0:T(128)} %constant.149) | copy-start | bytes 1540
  226.1 47.9 %copy-start.8 = (bf16[5,360,128]{2,1,0:T(8,128)(2,1)S(1)}, bf16[5,360,128]{2,1,0:T(8,128)(2,1)}, u32[]{:S(2)}) copy-start(bf16[5,360,128]{2,1,0:T(8,128)(2,1)} %copy-done.7) | copy-start | bytes 1382404
  227.5 50.0 %collective-permute-start.2 = (bf16[2,3,3,40,640]{4,3,2,1,0:T(8,128)(2,1)}, bf16[2,3,3,40,640]{4,3,2,1,0:T(8,128)(2,1)}, u32[]{:S(2)}, u32[]{:S(2)}) collective-permute-start(bf16[2,3,3,40,640]{4,3,2,1,0:T(8,128)(2,1)} %get-tuple-element.559), channel_id=1, source_target_pairs={{8,0},{16,8},{24,16},{32,24},{40,32},{48,40},{56,48},{64,56},{72,6... | collective-permute-start | bytes 2764808 | tf_op jit(solution)/shard_map/ppermute | solution.py:37
  228.8 48.7 %collective-permute-start.3 = (bf16[2,3,3,40,640]{4,3,2,1,0:T(8,128)(2,1)}, bf16[2,3,3,40,640]{4,3,2,1,0:T(8,128)(2,1)}, u32[]{:S(2)}, u32[]{:S(2)}) collective-permute-start(bf16[2,3,3,40,640]{4,3,2,1,0:T(8,128)(2,1)} %get-tuple-element.560), channel_id=1, source_target_pairs={{0,8},{8,16},{16,24},{24,32},{32,40},{40,48},{48,56},{56,64},{64,7... | collective-permute-start | bytes 2764808 | tf_op jit(solution)/shard_map/ppermute | solution.py:37
  277.5 123.3 %copy-start.1 = (bf16[3,3,40,640]{3,2,1,0:T(8,128)(2,1)S(1)}, bf16[3,3,40,640]{3,2,1,0:T(8,128)(2,1)}, u32[]{:S(2)}) copy-start(bf16[3,3,40,640]{3,2,1,0:T(8,128)(2,1)} %param.10) | copy-start | bytes 1382404
Sparse Core Ops, SparseCore 0:
  100.2 298.2 all-reduce.2
Sparse Core Ops, SparseCore 1:
  131.6 164.1 reduce-scatter.1
